TPU v7x, 128 devices: a whole 4x4x4 slice. The times are simulated.
128 devices in a mesh: grp: 16 (over x, y), chan: 8 (over z, core).
Axes of the slice: x: 4, y: 4, z: 4, core: 2. Of those that a mesh axis runs over, the one named last changes fastest.
Arguments:
- spectra: bfloat16 [2048, 2, 2, 8192], P(('grp', 'chan')), may hold values from -45 to 45
- pair_blocks: int32 [16, 8, 18, 2], P('grp', 'chan'), may hold values from 0 to 63
- owners: int32 [16, 8, 18, 1], P('grp', 'chan'), may hold values from 0 to 15; in each aligned block of 18 rows (0 to 17, 18 to 35, ..., all dimensions but the last counted through in order) at most 3 rows name the same one
Outputs:
- stacks: float32 [16, 8, 48, 4, 1024], P('grp', 'chan')
Inputs may be any that keep to these rules, and one draw needn't show every extreme that they name: `owners`: at most 3 of one device's 18 pair blocks name the same owner.
All inputs are finite; a program needn't handle non-finite values.
Results may differ from a plain program's by a relative error of at most 0.011.
Values may be sent and summed in bfloat16 or wider, within the bound.
A program may use at most 128 MiB of HBM per device.

v0:
```python
import jax
import jax.numpy as jnp
from jax import lax
from jax.sharding import PartitionSpec as P

F = 8192
LAGS = 1024
BLK = 2
NB_SRC = 18
MOST = 3
WINDOWS = 2


def table_block(start, count):
    bins = start + jnp.arange(count, dtype=jnp.int32)
    lag_index = jnp.arange(LAGS, dtype=jnp.int32) - LAGS // 2
    phase = bins[:, None] * lag_index[None, :] % (2 * F)
    angle = phase.astype(jnp.float32) * (jnp.pi / F)
    weight = jnp.where(bins == 0, 1.0, 2.0).astype(jnp.float32) / jnp.sqrt(jnp.float32(F))
    cos_part = (jnp.cos(angle) * weight[:, None]).astype(jnp.bfloat16)
    sin_part = (-jnp.sin(angle) * weight[:, None]).astype(jnp.bfloat16)
    return (cos_part, sin_part)


def to_lags(rows):
    width_block = min(512, F)
    real_rows = rows[:, 0]
    imag_rows = rows[:, 1]

    def add_block(turn, total):
        start = (turn * width_block).astype(jnp.int32)
        cos_part, sin_part = table_block(start, width_block)
        real_slice = lax.dynamic_slice_in_dim(real_rows, start, width_block, 1)
        imag_slice = lax.dynamic_slice_in_dim(imag_rows, start, width_block, 1)
        total = total + jnp.dot(real_slice, cos_part, preferred_element_type=jnp.float32)
        return total + jnp.dot(imag_slice, sin_part, preferred_element_type=jnp.float32)

    start_total = jnp.zeros((rows.shape[0], LAGS), jnp.float32)
    return lax.fori_loop(0, F // width_block, add_block, start_total)


def whiten(spectra):
    values = spectra.astype(jnp.float32)
    power = values[:, :, 0] ** 2 + values[:, :, 1] ** 2
    level = jnp.mean(power, axis=-1, keepdims=True) + 1e-05
    scale = lax.rsqrt(power + 0.1 * level)
    return (values * scale[:, :, None, :]).astype(jnp.bfloat16)


def cross_pairs(left, right):
    real_left = left[..., :, None, :, 0, :]
    imag_left = left[..., :, None, :, 1, :]
    real_right = right[..., None, :, :, 0, :]
    imag_right = right[..., None, :, :, 1, :]
    real_part = real_left * real_right + imag_left * imag_right
    imag_part = imag_left * real_right - real_left * imag_right
    both = jnp.stack([real_part, imag_part], axis=-2)
    return both.astype(jnp.bfloat16)


def local(spectra, pair_blocks, owners):
    groups_count = lax.axis_size("grp")
    slot_count = groups_count * MOST
    white = whiten(spectra)
    panel = lax.all_gather(white, "chan", axis=0, tiled=True)
    blocks = pair_blocks[0, 0]
    offsets = jnp.arange(BLK, dtype=jnp.int32)
    left_idx = blocks[:, 0][:, None] * BLK + offsets
    right_idx = blocks[:, 1][:, None] * BLK + offsets
    left = jnp.take(panel, left_idx, axis=0).astype(jnp.float32)
    right = jnp.take(panel, right_idx, axis=0).astype(jnp.float32)
    cross = cross_pairs(left, right).reshape(NB_SRC, BLK * BLK, WINDOWS, 2, F)
    owner_list = owners[0, 0, :, 0]
    same = owner_list[:, None] == owner_list[None, :]
    earlier = jnp.arange(NB_SRC)[None, :] < jnp.arange(NB_SRC)[:, None]
    order_rank = jnp.sum(jnp.logical_and(same, earlier), axis=1)
    slot_ids = owner_list * MOST + order_rank
    chooser = slot_ids[None, :] == jnp.arange(slot_count, dtype=jnp.int32)[:, None]
    pairs = BLK * BLK
    summed = jnp.zeros((groups_count, MOST, pairs, 2, F), jnp.float32)
    for window in range(WINDOWS):
        placed = jnp.einsum(
            "ms,sprf->mprf",
            chooser.astype(jnp.bfloat16),
            cross[:, :, window],
            preferred_element_type=jnp.float32,
        )
        summed = summed + lax.all_to_all(
            placed.astype(jnp.bfloat16).reshape(groups_count, MOST, pairs, 2, F),
            "grp",
            split_axis=0,
            concat_axis=0,
            tiled=True,
        ).astype(jnp.float32)
    received = (summed / WINDOWS).astype(jnp.bfloat16)
    shape_now = received.shape
    rows = received.reshape(-1, 2, F)
    result = to_lags(rows).reshape(shape_now[0], shape_now[1], pairs, LAGS)
    return result.reshape(1, 1, slot_count, pairs, LAGS)


def solution(mesh):
    return jax.shard_map(
        local,
        mesh=mesh,
        in_specs=(
            P(("grp", "chan"), None, None, None),
            P("grp", "chan", None, None),
            P("grp", "chan", None, None),
        ),
        out_specs=P("grp", "chan", None, None, None),
        check_vma=False,
    )
```

profile of v0, /device:TPU:20, one launch (start us, length us, event | category | flops | bytes accessed | tf_op | source)
XLA Modules:
  0.0 685.6 jit_solution(13492980502422854776)
XLA Ops:
  6.5 1.8 copy_convert_fusion
  8.6 0.3 rsqrt_bitcast_fusion
  8.9 0.7 copy-done.3
  9.6 0.6 multiply_convert_fusion.5
  10.2 2.1 copy.50
  13.3 51.4 %all-gather.2.cloned.1.call-done = bf16[128,2,2,8192]{3,2,1,0:T(2,128)(2,1)} async-done(((bf16[16,2,2,8192]{3,2,1,0:T(2,128)(2,1)}), bf16[128,2,2,8192]{3,2,1,0:T(2,128)(2,1)}) %all-gather.2.cloned.1.call-update) | async-done | bytes 8388624 | tf_op jit(solution)/shard_map/all_gather | solution.py:65
  64.7 11.3 %gather_fusion = bf16[36,2,2,8192]{3,2,1,0:T(2,128)(2,1)S(1)} fusion(bf16[128,2,2,8192]{3,2,1,0:T(2,128)(2,1)} %all-gather.2.cloned.1.call-done, s32[1024]{0:T(1024)S(1)} %pad_clamp_fusion.1), kind=kCustom, calls=%fused_computation.clone | custom fusion | bytes 4718736 | tf_op jit(solution)/shard_map/jit(_take)/gather | solution.py:70
  75.9 2.1 fusion.23
  78.1 5.4 fusion.36
  83.5 3.3 copy.81
  86.7 3.3 copy.83
  90.0 11.5 %gather_fusion.1 = bf16[36,2,2,8192]{3,2,1,0:T(2,128)(2,1)S(1)} fusion(bf16[128,2,2,8192]{3,2,1,0:T(2,128)(2,1)} %all-gather.2.cloned.1.call-done, s32[1024]{0:T(1024)S(1)} %pad_clamp_fusion), kind=kCustom, calls=%fused_computation.1.clone | custom fusion | bytes 4718736 | tf_op jit(solution)/shard_map/jit(_take)/gather | solution.py:71
  101.5 2.1 fusion.24
  103.6 5.4 fusion.37
  109.0 1.5 copy.80
  110.6 1.5 copy.82
  112.1 0.4 copy-done.1
  112.5 1.7 add_convert_fusion
  114.2 2.2 convolution_convert_fusion.1
  116.5 11.0 %copy.58 = bf16[48,4,2,8192]{3,2,1,0:T(2,128)(2,1)} copy(bf16[48,4,2,8192]{3,0,2,1:T(8,128)(2,1)S(1)} %convolution_convert_fusion.1) | data formatting | bytes 12582912 | tf_op jit(solution)/shard_map/convert_element_type | solution.py:89
  127.5 7.2 %all-to-all-start = ((bf16[16,3,4,2,8192]{4,3,2,1,0:T(2,128)(2,1)}), bf16[16,3,4,2,8192]{4,3,2,1,0:T(2,128)(2,1)}, u32[]{:S(2)}, u32[]{:S(2)}) async-start(bf16[16,3,4,2,8192]{4,3,2,1,0:T(2,128)(2,1)} %bitcast.52), calls=%async_computation | async-start | bytes 12582912 | tf_op jit(solution)/shard_map/all_to_all | solution.py:88
  134.7 3.3 convolution_convert_fusion
  138.0 11.0 %copy.59 = bf16[48,4,2,8192]{3,2,1,0:T(2,128)(2,1)} copy(bf16[48,4,2,8192]{3,0,2,1:T(8,128)(2,1)S(1)} %convolution_convert_fusion) | data formatting | bytes 12582912 | tf_op jit(solution)/shard_map/convert_element_type | solution.py:89
  149.0 89.4 %all-to-all-done = bf16[16,3,4,2,8192]{4,3,2,1,0:T(2,128)(2,1)} async-done(((bf16[16,3,4,2,8192]{4,3,2,1,0:T(2,128)(2,1)}), bf16[16,3,4,2,8192]{4,3,2,1,0:T(2,128)(2,1)}, u32[]{:S(2)}, u32[]{:S(2)}) %all-to-all-start) | async-done | bytes 6291488 | tf_op jit(solution)/shard_map/all_to_all | solution.py:88
  238.5 14.3 %all-to-all-start.1 = ((bf16[16,3,4,2,8192]{4,3,2,1,0:T(2,128)(2,1)}), bf16[16,3,4,2,8192]{4,3,2,1,0:T(2,128)(2,1)}, u32[]{:S(2)}, u32[]{:S(2)}) async-start(bf16[16,3,4,2,8192]{4,3,2,1,0:T(2,128)(2,1)} %bitcast.51), calls=%async_computation.1 | async-start | bytes 12582912 | tf_op jit(solution)/shard_map/all_to_all | solution.py:88
  252.8 99.9 %all-to-all-done.1 = bf16[16,3,4,2,8192]{4,3,2,1,0:T(2,128)(2,1)} async-done(((bf16[16,3,4,2,8192]{4,3,2,1,0:T(2,128)(2,1)}), bf16[16,3,4,2,8192]{4,3,2,1,0:T(2,128)(2,1)}, u32[]{:S(2)}, u32[]{:S(2)}) %all-to-all-start.1) | async-done | bytes 6291488 | tf_op jit(solution)/shard_map/all_to_all | solution.py:88
  352.7 11.2 %multiply_convert_fusion.4 = bf16[16,3,4,2,8192]{4,3,2,1,0:T(2,128)(2,1)S(1)} fusion(bf16[16,3,4,2,8192]{4,3,2,1,0:T(2,128)(2,1)} %all-to-all-done.1, bf16[16,3,4,2,8192]{4,3,2,1,0:T(2,128)(2,1)} %all-to-all-done), kind=kLoop, calls=%fused_computation.29 | loop fusion | flops 15728640 | bytes 18874368 | tf_op jit(solution)/shard_map/convert_element_type | solution.py:95
  363.9 13.4 %fusion.35 = (bf16[192,1,8192]{2,1,0:T(2,128)(2,1)S(1)}, bf16[192,1,8192]{2,1,0:T(2,128)(2,1)S(1)}) fusion(bf16[192,2,8192]{2,1,0:T(2,128)(2,1)S(1)} %bitcast.46), kind=kLoop, calls=%fused_computation.77 | loop fusion | bytes 12582912 | tf_op jit(solution)/shard_map/slice | solution.py:28
  377.3 3.4 copy.78
  380.8 5.1 copy.79
  385.9 290.4 %while.16 = (s32[]{:T(128)}, f32[192,1024]{1,0:T(8,128)}, bf16[192,8192]{1,0:T(8,128)(2,1)}, bf16[192,8192]{1,0:T(8,128)(2,1)S(1)}, s32[]{:T(128)}, /*index=5*/s32[]{:T(128)}, s32[]{:T(128)}, s32[]{:T(128)}) while((s32[]{:T(128)}, f32[192,1024]{1,0:T(8,128)}, bf16[192,8192]{1,0:T(8,128)(2,1)}, bf16[192,8192]{1,0:T(8,128)(2,1)S(1)}, ...), condition=%wide.region_3.5_spmd.clone, body=%wide.region_2.4_spmd.clone.sunk | while | flops 420548096 | bytes 3563677 | solution.py:39
  386.1 8.9 %convolution_add_fusion.4 = f32[192,1024]{1,0:T(8,128)S(1)} fusion(f32[512]{0:T(512)S(1)} %select_multiply_fusion.2, s32[1024]{0:T(1024)S(1)} %iota_add_fusion.4, s32[512]{0:T(512)S(1)} %iota_add_fusion.5, f32[192,1024]{1,0:T(8,128)} %get-tuple-element.190, pred[]{:T(512)S(6)} %compare.4, bf16[192,8192]{1,0:T(8,128)(2,1)} %get-tuple-element.199, ...), kind=kOutput, calls=%fused_computation.13.clone.1 | convolution fusion | flops 210108416 | bytes 1777669 | tf_op jit(solution)/shard_map/while/body/eval_jaxpr/dot_general | solution.py:35
  395.0 9.0 %convolution_add_fusion.5 = f32[192,1024]{1,0:T(8,128)} fusion(f32[192,1024]{1,0:T(8,128)S(1)} %convolution_add_fusion.4, f32[512]{0:T(512)S(1)} %select_multiply_fusion.2, s32[1024]{0:T(1024)S(1)} %iota_add_fusion.4, s32[512]{0:T(512)S(1)} %iota_add_fusion.5, bf16[192,8192]{1,0:T(8,128)(2,1)S(1)} %get-tuple-element.200, s32[]{:T(128)S(6)} %select_n.93), kind=kOutput, calls=%fused_computation.12.clone.1 | convolution fusion | flops 210436096 | bytes 1777668 | tf_op jit(solution)/shard_map/while/body/eval_jaxpr/dot_general | solution.py:36
  403.9 9.2 %convolution_add_fusion.4 = f32[192,1024]{1,0:T(8,128)S(1)} fusion(f32[512]{0:T(512)S(1)} %select_multiply_fusion.2, s32[1024]{0:T(1024)S(1)} %iota_add_fusion.4, s32[512]{0:T(512)S(1)} %iota_add_fusion.5, f32[192,1024]{1,0:T(8,128)} %get-tuple-element.190, pred[]{:T(512)S(6)} %compare.4, bf16[192,8192]{1,0:T(8,128)(2,1)} %get-tuple-element.199, ...), kind=kOutput, calls=%fused_computation.13.clone.1 | convolution fusion | flops 210108416 | bytes 1777669 | tf_op jit(solution)/shard_map/while/body/eval_jaxpr/dot_general | solution.py:35
  413.1 9.0 %convolution_add_fusion.5 = f32[192,1024]{1,0:T(8,128)} fusion(f32[192,1024]{1,0:T(8,128)S(1)} %convolution_add_fusion.4, f32[512]{0:T(512)S(1)} %select_multiply_fusion.2, s32[1024]{0:T(1024)S(1)} %iota_add_fusion.4, s32[512]{0:T(512)S(1)} %iota_add_fusion.5, bf16[192,8192]{1,0:T(8,128)(2,1)S(1)} %get-tuple-element.200, s32[]{:T(128)S(6)} %select_n.93), kind=kOutput, calls=%fused_computation.12.clone.1 | convolution fusion | flops 210436096 | bytes 1777668 | tf_op jit(solution)/shard_map/while/body/eval_jaxpr/dot_general | solution.py:36
  422.1 9.2 %convolution_add_fusion.4 = f32[192,1024]{1,0:T(8,128)S(1)} fusion(f32[512]{0:T(512)S(1)} %select_multiply_fusion.2, s32[1024]{0:T(1024)S(1)} %iota_add_fusion.4, s32[512]{0:T(512)S(1)} %iota_add_fusion.5, f32[192,1024]{1,0:T(8,128)} %get-tuple-element.190, pred[]{:T(512)S(6)} %compare.4, bf16[192,8192]{1,0:T(8,128)(2,1)} %get-tuple-element.199, ...), kind=kOutput, calls=%fused_computation.13.clone.1 | convolution fusion | flops 210108416 | bytes 1777669 | tf_op jit(solution)/shard_map/while/body/eval_jaxpr/dot_general | solution.py:35
  431.3 9.0 %convolution_add_fusion.5 = f32[192,1024]{1,0:T(8,128)} fusion(f32[192,1024]{1,0:T(8,128)S(1)} %convolution_add_fusion.4, f32[512]{0:T(512)S(1)} %select_multiply_fusion.2, s32[1024]{0:T(1024)S(1)} %iota_add_fusion.4, s32[512]{0:T(512)S(1)} %iota_add_fusion.5, bf16[192,8192]{1,0:T(8,128)(2,1)S(1)} %get-tuple-element.200, s32[]{:T(128)S(6)} %select_n.93), kind=kOutput, calls=%fused_computation.12.clone.1 | convolution fusion | flops 210436096 | bytes 1777668 | tf_op jit(solution)/shard_map/while/body/eval_jaxpr/dot_general | solution.py:36
  440.2 9.2 %convolution_add_fusion.4 = f32[192,1024]{1,0:T(8,128)S(1)} fusion(f32[512]{0:T(512)S(1)} %select_multiply_fusion.2, s32[1024]{0:T(1024)S(1)} %iota_add_fusion.4, s32[512]{0:T(512)S(1)} %iota_add_fusion.5, f32[192,1024]{1,0:T(8,128)} %get-tuple-element.190, pred[]{:T(512)S(6)} %compare.4, bf16[192,8192]{1,0:T(8,128)(2,1)} %get-tuple-element.199, ...), kind=kOutput, calls=%fused_computation.13.clone.1 | convolution fusion | flops 210108416 | bytes 1777669 | tf_op jit(solution)/shard_map/while/body/eval_jaxpr/dot_general | solution.py:35
  449.4 9.0 %convolution_add_fusion.5 = f32[192,1024]{1,0:T(8,128)} fusion(f32[192,1024]{1,0:T(8,128)S(1)} %convolution_add_fusion.4, f32[512]{0:T(512)S(1)} %select_multiply_fusion.2, s32[1024]{0:T(1024)S(1)} %iota_add_fusion.4, s32[512]{0:T(512)S(1)} %iota_add_fusion.5, bf16[192,8192]{1,0:T(8,128)(2,1)S(1)} %get-tuple-element.200, s32[]{:T(128)S(6)} %select_n.93), kind=kOutput, calls=%fused_computation.12.clone.1 | convolution fusion | flops 210436096 | bytes 1777668 | tf_op jit(solution)/shard_map/while/body/eval_jaxpr/dot_general | solution.py:36
  458.4 9.2 %convolution_add_fusion.4 = f32[192,1024]{1,0:T(8,128)S(1)} fusion(f32[512]{0:T(512)S(1)} %select_multiply_fusion.2, s32[1024]{0:T(1024)S(1)} %iota_add_fusion.4, s32[512]{0:T(512)S(1)} %iota_add_fusion.5, f32[192,1024]{1,0:T(8,128)} %get-tuple-element.190, pred[]{:T(512)S(6)} %compare.4, bf16[192,8192]{1,0:T(8,128)(2,1)} %get-tuple-element.199, ...), kind=kOutput, calls=%fused_computation.13.clone.1 | convolution fusion | flops 210108416 | bytes 1777669 | tf_op jit(solution)/shard_map/while/body/eval_jaxpr/dot_general | solution.py:35
  467.6 9.0 %convolution_add_fusion.5 = f32[192,1024]{1,0:T(8,128)} fusion(f32[192,1024]{1,0:T(8,128)S(1)} %convolution_add_fusion.4, f32[512]{0:T(512)S(1)} %select_multiply_fusion.2, s32[1024]{0:T(1024)S(1)} %iota_add_fusion.4, s32[512]{0:T(512)S(1)} %iota_add_fusion.5, bf16[192,8192]{1,0:T(8,128)(2,1)S(1)} %get-tuple-element.200, s32[]{:T(128)S(6)} %select_n.93), kind=kOutput, calls=%fused_computation.12.clone.1 | convolution fusion | flops 210436096 | bytes 1777668 | tf_op jit(solution)/shard_map/while/body/eval_jaxpr/dot_general | solution.py:36
  476.6 9.2 %convolution_add_fusion.4 = f32[192,1024]{1,0:T(8,128)S(1)} fusion(f32[512]{0:T(512)S(1)} %select_multiply_fusion.2, s32[1024]{0:T(1024)S(1)} %iota_add_fusion.4, s32[512]{0:T(512)S(1)} %iota_add_fusion.5, f32[192,1024]{1,0:T(8,128)} %get-tuple-element.190, pred[]{:T(512)S(6)} %compare.4, bf16[192,8192]{1,0:T(8,128)(2,1)} %get-tuple-element.199, ...), kind=kOutput, calls=%fused_computation.13.clone.1 | convolution fusion | flops 210108416 | bytes 1777669 | tf_op jit(solution)/shard_map/while/body/eval_jaxpr/dot_general | solution.py:35
  485.7 9.0 %convolution_add_fusion.5 = f32[192,1024]{1,0:T(8,128)} fusion(f32[192,1024]{1,0:T(8,128)S(1)} %convolution_add_fusion.4, f32[512]{0:T(512)S(1)} %select_multiply_fusion.2, s32[1024]{0:T(1024)S(1)} %iota_add_fusion.4, s32[512]{0:T(512)S(1)} %iota_add_fusion.5, bf16[192,8192]{1,0:T(8,128)(2,1)S(1)} %get-tuple-element.200, s32[]{:T(128)S(6)} %select_n.93), kind=kOutput, calls=%fused_computation.12.clone.1 | convolution fusion | flops 210436096 | bytes 1777668 | tf_op jit(solution)/shard_map/while/body/eval_jaxpr/dot_general | solution.py:36
  494.7 9.2 %convolution_add_fusion.4 = f32[192,1024]{1,0:T(8,128)S(1)} fusion(f32[512]{0:T(512)S(1)} %select_multiply_fusion.2, s32[1024]{0:T(1024)S(1)} %iota_add_fusion.4, s32[512]{0:T(512)S(1)} %iota_add_fusion.5, f32[192,1024]{1,0:T(8,128)} %get-tuple-element.190, pred[]{:T(512)S(6)} %compare.4, bf16[192,8192]{1,0:T(8,128)(2,1)} %get-tuple-element.199, ...), kind=kOutput, calls=%fused_computation.13.clone.1 | convolution fusion | flops 210108416 | bytes 1777669 | tf_op jit(solution)/shard_map/while/body/eval_jaxpr/dot_general | solution.py:35
  503.9 9.0 %convolution_add_fusion.5 = f32[192,1024]{1,0:T(8,128)} fusion(f32[192,1024]{1,0:T(8,128)S(1)} %convolution_add_fusion.4, f32[512]{0:T(512)S(1)} %select_multiply_fusion.2, s32[1024]{0:T(1024)S(1)} %iota_add_fusion.4, s32[512]{0:T(512)S(1)} %iota_add_fusion.5, bf16[192,8192]{1,0:T(8,128)(2,1)S(1)} %get-tuple-element.200, s32[]{:T(128)S(6)} %select_n.93), kind=kOutput, calls=%fused_computation.12.clone.1 | convolution fusion | flops 210436096 | bytes 1777668 | tf_op jit(solution)/shard_map/while/body/eval_jaxpr/dot_general | solution.py:36
  512.9 9.2 %convolution_add_fusion.4 = f32[192,1024]{1,0:T(8,128)S(1)} fusion(f32[512]{0:T(512)S(1)} %select_multiply_fusion.2, s32[1024]{0:T(1024)S(1)} %iota_add_fusion.4, s32[512]{0:T(512)S(1)} %iota_add_fusion.5, f32[192,1024]{1,0:T(8,128)} %get-tuple-element.190, pred[]{:T(512)S(6)} %compare.4, bf16[192,8192]{1,0:T(8,128)(2,1)} %get-tuple-element.199, ...), kind=kOutput, calls=%fused_computation.13.clone.1 | convolution fusion | flops 210108416 | bytes 1777669 | tf_op jit(solution)/shard_map/while/body/eval_jaxpr/dot_general | solution.py:35
  522.1 9.0 %convolution_add_fusion.5 = f32[192,1024]{1,0:T(8,128)} fusion(f32[192,1024]{1,0:T(8,128)S(1)} %convolution_add_fusion.4, f32[512]{0:T(512)S(1)} %select_multiply_fusion.2, s32[1024]{0:T(1024)S(1)} %iota_add_fusion.4, s32[512]{0:T(512)S(1)} %iota_add_fusion.5, bf16[192,8192]{1,0:T(8,128)(2,1)S(1)} %get-tuple-element.200, s32[]{:T(128)S(6)} %select_n.93), kind=kOutput, calls=%fused_computation.12.clone.1 | convolution fusion | flops 210436096 | bytes 1777668 | tf_op jit(solution)/shard_map/while/body/eval_jaxpr/dot_general | solution.py:36
  531.0 9.2 %convolution_add_fusion.4 = f32[192,1024]{1,0:T(8,128)S(1)} fusion(f32[512]{0:T(512)S(1)} %select_multiply_fusion.2, s32[1024]{0:T(1024)S(1)} %iota_add_fusion.4, s32[512]{0:T(512)S(1)} %iota_add_fusion.5, f32[192,1024]{1,0:T(8,128)} %get-tuple-element.190, pred[]{:T(512)S(6)} %compare.4, bf16[192,8192]{1,0:T(8,128)(2,1)} %get-tuple-element.199, ...), kind=kOutput, calls=%fused_computation.13.clone.1 | convolution fusion | flops 210108416 | bytes 1777669 | tf_op jit(solution)/shard_map/while/body/eval_jaxpr/dot_general | solution.py:35
  540.2 9.0 %convolution_add_fusion.5 = f32[192,1024]{1,0:T(8,128)} fusion(f32[192,1024]{1,0:T(8,128)S(1)} %convolution_add_fusion.4, f32[512]{0:T(512)S(1)} %select_multiply_fusion.2, s32[1024]{0:T(1024)S(1)} %iota_add_fusion.4, s32[512]{0:T(512)S(1)} %iota_add_fusion.5, bf16[192,8192]{1,0:T(8,128)(2,1)S(1)} %get-tuple-element.200, s32[]{:T(128)S(6)} %select_n.93), kind=kOutput, calls=%fused_computation.12.clone.1 | convolution fusion | flops 210436096 | bytes 1777668 | tf_op jit(solution)/shard_map/while/body/eval_jaxpr/dot_general | solution.py:36
  549.2 9.2 %convolution_add_fusion.4 = f32[192,1024]{1,0:T(8,128)S(1)} fusion(f32[512]{0:T(512)S(1)} %select_multiply_fusion.2, s32[1024]{0:T(1024)S(1)} %iota_add_fusion.4, s32[512]{0:T(512)S(1)} %iota_add_fusion.5, f32[192,1024]{1,0:T(8,128)} %get-tuple-element.190, pred[]{:T(512)S(6)} %compare.4, bf16[192,8192]{1,0:T(8,128)(2,1)} %get-tuple-element.199, ...), kind=kOutput, calls=%fused_computation.13.clone.1 | convolution fusion | flops 210108416 | bytes 1777669 | tf_op jit(solution)/shard_map/while/body/eval_jaxpr/dot_general | solution.py:35
  558.4 9.0 %convolution_add_fusion.5 = f32[192,1024]{1,0:T(8,128)} fusion(f32[192,1024]{1,0:T(8,128)S(1)} %convolution_add_fusion.4, f32[512]{0:T(512)S(1)} %select_multiply_fusion.2, s32[1024]{0:T(1024)S(1)} %iota_add_fusion.4, s32[512]{0:T(512)S(1)} %iota_add_fusion.5, bf16[192,8192]{1,0:T(8,128)(2,1)S(1)} %get-tuple-element.200, s32[]{:T(128)S(6)} %select_n.93), kind=kOutput, calls=%fused_computation.12.clone.1 | convolution fusion | flops 210436096 | bytes 1777668 | tf_op jit(solution)/shard_map/while/body/eval_jaxpr/dot_general | solution.py:36
  567.3 9.2 %convolution_add_fusion.4 = f32[192,1024]{1,0:T(8,128)S(1)} fusion(f32[512]{0:T(512)S(1)} %select_multiply_fusion.2, s32[1024]{0:T(1024)S(1)} %iota_add_fusion.4, s32[512]{0:T(512)S(1)} %iota_add_fusion.5, f32[192,1024]{1,0:T(8,128)} %get-tuple-element.190, pred[]{:T(512)S(6)} %compare.4, bf16[192,8192]{1,0:T(8,128)(2,1)} %get-tuple-element.199, ...), kind=kOutput, calls=%fused_computation.13.clone.1 | convolution fusion | flops 210108416 | bytes 1777669 | tf_op jit(solution)/shard_map/while/body/eval_jaxpr/dot_general | solution.py:35
  576.5 9.0 %convolution_add_fusion.5 = f32[192,1024]{1,0:T(8,128)} fusion(f32[192,1024]{1,0:T(8,128)S(1)} %convolution_add_fusion.4, f32[512]{0:T(512)S(1)} %select_multiply_fusion.2, s32[1024]{0:T(1024)S(1)} %iota_add_fusion.4, s32[512]{0:T(512)S(1)} %iota_add_fusion.5, bf16[192,8192]{1,0:T(8,128)(2,1)S(1)} %get-tuple-element.200, s32[]{:T(128)S(6)} %select_n.93), kind=kOutput, calls=%fused_computation.12.clone.1 | convolution fusion | flops 210436096 | bytes 1777668 | tf_op jit(solution)/shard_map/while/body/eval_jaxpr/dot_general | solution.py:36
  585.5 9.2 %convolution_add_fusion.4 = f32[192,1024]{1,0:T(8,128)S(1)} fusion(f32[512]{0:T(512)S(1)} %select_multiply_fusion.2, s32[1024]{0:T(1024)S(1)} %iota_add_fusion.4, s32[512]{0:T(512)S(1)} %iota_add_fusion.5, f32[192,1024]{1,0:T(8,128)} %get-tuple-element.190, pred[]{:T(512)S(6)} %compare.4, bf16[192,8192]{1,0:T(8,128)(2,1)} %get-tuple-element.199, ...), kind=kOutput, calls=%fused_computation.13.clone.1 | convolution fusion | flops 210108416 | bytes 1777669 | tf_op jit(solution)/shard_map/while/body/eval_jaxpr/dot_general | solution.py:35
  594.7 9.0 %convolution_add_fusion.5 = f32[192,1024]{1,0:T(8,128)} fusion(f32[192,1024]{1,0:T(8,128)S(1)} %convolution_add_fusion.4, f32[512]{0:T(512)S(1)} %select_multiply_fusion.2, s32[1024]{0:T(1024)S(1)} %iota_add_fusion.4, s32[512]{0:T(512)S(1)} %iota_add_fusion.5, bf16[192,8192]{1,0:T(8,128)(2,1)S(1)} %get-tuple-element.200, s32[]{:T(128)S(6)} %select_n.93), kind=kOutput, calls=%fused_computation.12.clone.1 | convolution fusion | flops 210436096 | bytes 1777668 | tf_op jit(solution)/shard_map/while/body/eval_jaxpr/dot_general | solution.py:36
  603.6 9.2 %convolution_add_fusion.4 = f32[192,1024]{1,0:T(8,128)S(1)} fusion(f32[512]{0:T(512)S(1)} %select_multiply_fusion.2, s32[1024]{0:T(1024)S(1)} %iota_add_fusion.4, s32[512]{0:T(512)S(1)} %iota_add_fusion.5, f32[192,1024]{1,0:T(8,128)} %get-tuple-element.190, pred[]{:T(512)S(6)} %compare.4, bf16[192,8192]{1,0:T(8,128)(2,1)} %get-tuple-element.199, ...), kind=kOutput, calls=%fused_computation.13.clone.1 | convolution fusion | flops 210108416 | bytes 1777669 | tf_op jit(solution)/shard_map/while/body/eval_jaxpr/dot_general | solution.py:35
  612.8 9.0 %convolution_add_fusion.5 = f32[192,1024]{1,0:T(8,128)} fusion(f32[192,1024]{1,0:T(8,128)S(1)} %convolution_add_fusion.4, f32[512]{0:T(512)S(1)} %select_multiply_fusion.2, s32[1024]{0:T(1024)S(1)} %iota_add_fusion.4, s32[512]{0:T(512)S(1)} %iota_add_fusion.5, bf16[192,8192]{1,0:T(8,128)(2,1)S(1)} %get-tuple-element.200, s32[]{:T(128)S(6)} %select_n.93), kind=kOutput, calls=%fused_computation.12.clone.1 | convolution fusion | flops 210436096 | bytes 1777668 | tf_op jit(solution)/shard_map/while/body/eval_jaxpr/dot_general | solution.py:36
  621.8 9.2 %convolution_add_fusion.4 = f32[192,1024]{1,0:T(8,128)S(1)} fusion(f32[512]{0:T(512)S(1)} %select_multiply_fusion.2, s32[1024]{0:T(1024)S(1)} %iota_add_fusion.4, s32[512]{0:T(512)S(1)} %iota_add_fusion.5, f32[192,1024]{1,0:T(8,128)} %get-tuple-element.190, pred[]{:T(512)S(6)} %compare.4, bf16[192,8192]{1,0:T(8,128)(2,1)} %get-tuple-element.199, ...), kind=kOutput, calls=%fused_computation.13.clone.1 | convolution fusion | flops 210108416 | bytes 1777669 | tf_op jit(solution)/shard_map/while/body/eval_jaxpr/dot_general | solution.py:35
  631.0 9.0 %convolution_add_fusion.5 = f32[192,1024]{1,0:T(8,128)} fusion(f32[192,1024]{1,0:T(8,128)S(1)} %convolution_add_fusion.4, f32[512]{0:T(512)S(1)} %select_multiply_fusion.2, s32[1024]{0:T(1024)S(1)} %iota_add_fusion.4, s32[512]{0:T(512)S(1)} %iota_add_fusion.5, bf16[192,8192]{1,0:T(8,128)(2,1)S(1)} %get-tuple-element.200, s32[]{:T(128)S(6)} %select_n.93), kind=kOutput, calls=%fused_computation.12.clone.1 | convolution fusion | flops 210436096 | bytes 1777668 | tf_op jit(solution)/shard_map/while/body/eval_jaxpr/dot_general | solution.py:36
  640.0 9.2 %convolution_add_fusion.4 = f32[192,1024]{1,0:T(8,128)S(1)} fusion(f32[512]{0:T(512)S(1)} %select_multiply_fusion.2, s32[1024]{0:T(1024)S(1)} %iota_add_fusion.4, s32[512]{0:T(512)S(1)} %iota_add_fusion.5, f32[192,1024]{1,0:T(8,128)} %get-tuple-element.190, pred[]{:T(512)S(6)} %compare.4, bf16[192,8192]{1,0:T(8,128)(2,1)} %get-tuple-element.199, ...), kind=kOutput, calls=%fused_computation.13.clone.1 | convolution fusion | flops 210108416 | bytes 1777669 | tf_op jit(solution)/shard_map/while/body/eval_jaxpr/dot_general | solution.py:35
  649.1 9.0 %convolution_add_fusion.5 = f32[192,1024]{1,0:T(8,128)} fusion(f32[192,1024]{1,0:T(8,128)S(1)} %convolution_add_fusion.4, f32[512]{0:T(512)S(1)} %select_multiply_fusion.2, s32[1024]{0:T(1024)S(1)} %iota_add_fusion.4, s32[512]{0:T(512)S(1)} %iota_add_fusion.5, bf16[192,8192]{1,0:T(8,128)(2,1)S(1)} %get-tuple-element.200, s32[]{:T(128)S(6)} %select_n.93), kind=kOutput, calls=%fused_computation.12.clone.1 | convolution fusion | flops 210436096 | bytes 1777668 | tf_op jit(solution)/shard_map/while/body/eval_jaxpr/dot_general | solution.py:36
  658.1 9.2 %convolution_add_fusion.4 = f32[192,1024]{1,0:T(8,128)S(1)} fusion(f32[512]{0:T(512)S(1)} %select_multiply_fusion.2, s32[1024]{0:T(1024)S(1)} %iota_add_fusion.4, s32[512]{0:T(512)S(1)} %iota_add_fusion.5, f32[192,1024]{1,0:T(8,128)} %get-tuple-element.190, pred[]{:T(512)S(6)} %compare.4, bf16[192,8192]{1,0:T(8,128)(2,1)} %get-tuple-element.199, ...), kind=kOutput, calls=%fused_computation.13.clone.1 | convolution fusion | flops 210108416 | bytes 1777669 | tf_op jit(solution)/shard_map/while/body/eval_jaxpr/dot_general | solution.py:35
  667.3 9.0 %convolution_add_fusion.5 = f32[192,1024]{1,0:T(8,128)} fusion(f32[192,1024]{1,0:T(8,128)S(1)} %convolution_add_fusion.4, f32[512]{0:T(512)S(1)} %select_multiply_fusion.2, s32[1024]{0:T(1024)S(1)} %iota_add_fusion.4, s32[512]{0:T(512)S(1)} %iota_add_fusion.5, bf16[192,8192]{1,0:T(8,128)(2,1)S(1)} %get-tuple-element.200, s32[]{:T(128)S(6)} %select_n.93), kind=kOutput, calls=%fused_computation.12.clone.1 | convolution fusion | flops 210436096 | bytes 1777668 | tf_op jit(solution)/shard_map/while/body/eval_jaxpr/dot_general | solution.py:36
  676.3 2.2 reshape_reshape.3
  (76 shorter events, 1.3 us)
Async XLA Ops:
  6.5 58.1 %all-gather.2.cloned.1.call-start = ((), (), s32[]{:S(2)}) async-start(), calls=%async_computation.2 | async-start | bytes 9437184 | tf_op jit(solution)/shard_map/all_gather | solution.py:65
  8.4 1.2 copy-start.3
  9.6 2.8 copy-start.4
  9.6 3.5 copy-start.5
  109.0 3.1 copy-start.2
  110.6 2.0 copy-start.1
  114.2 2.2 copy-start
  127.5 111.0 %all-to-all-start = ((bf16[16,3,4,2,8192]{4,3,2,1,0:T(2,128)(2,1)}), bf16[16,3,4,2,8192]{4,3,2,1,0:T(2,128)(2,1)}, u32[]{:S(2)}, u32[]{:S(2)}) async-start(bf16[16,3,4,2,8192]{4,3,2,1,0:T(2,128)(2,1)} %bitcast.52), calls=%async_computation | async-start | bytes 12582912 | tf_op jit(solution)/shard_map/all_to_all | solution.py:88
  238.5 114.2 %all-to-all-start.1 = ((bf16[16,3,4,2,8192]{4,3,2,1,0:T(2,128)(2,1)}), bf16[16,3,4,2,8192]{4,3,2,1,0:T(2,128)(2,1)}, u32[]{:S(2)}, u32[]{:S(2)}) async-start(bf16[16,3,4,2,8192]{4,3,2,1,0:T(2,128)(2,1)} %bitcast.51), calls=%async_computation.1 | async-start | bytes 12582912 | tf_op jit(solution)/shard_map/all_to_all | solution.py:88
Sparse Core Ops, SparseCore 0:
  12.5 52.0 all-gather.1
where the time goes:
time: 689 us; the launch traced here: 686 us
  matrix products  295 us (43%)
  waiting for transfers between devices  241 us (35%)
  local copies, waits for them, and re-layouts  93.2 us (14%)
  starting transfers between devices  21.5 us (3%)
  other arithmetic  20.5 us (3%)
  between operations  13.8 us (2%)
    all_to_all x2, waiting for transfers between devices, local(): lax.all_to_all(placed.astype(jnp.bfloat16).reshape(groups_count, MOST, pa...  189 us
    dot_general x16, matrix products, add_block(): jnp.dot(real_slice, cos_part, preferred_element_type=jnp.float32)  146 us
    dot_general x16, matrix products, add_block(): jnp.dot(imag_slice, sin_part, preferred_element_type=jnp.float32)  143 us
    all_gather x1, waiting for transfers between devices, local(): panel = lax.all_gather(white, 'chan', axis=0, tiled=True)  51.4 us
    convert_element_type x2, local copies, waits for them, and re-layouts, local(): placed.astype(jnp.bfloat16).reshape(groups_count, MOST, pairs, 2, F)  22 us
    all_to_all x2, starting transfers between devices, local(): lax.all_to_all(placed.astype(jnp.bfloat16).reshape(groups_count, MOST, pa...  21.5 us
  transfers between devices with their start and end apart: 3, of which 3 were waited for; matrix products, arithmetic and copies ran while one was open for 2% of the time, Pallas kernels for 0%

commit v1 on v0

--- a/solution.py
+++ b/solution.py
@@ -62,7 +62,12 @@
     groups_count = lax.axis_size("grp")
     slot_count = groups_count * MOST
     white = whiten(spectra)
-    panel = lax.all_gather(white, "chan", axis=0, tiled=True)
+    ring = [white]
+    for hop in range(7):
+        ring.append(lax.ppermute(ring[-1], "chan", [(dev, (dev + 1) % 8) for dev in range(8)]))
+    panel = jnp.roll(
+        jnp.concatenate(ring[::-1], axis=0), (lax.axis_index("chan") + 1) * ring[0].shape[0], axis=0
+    )
     blocks = pair_blocks[0, 0]
     offsets = jnp.arange(BLK, dtype=jnp.int32)
     left_idx = blocks[:, 0][:, None] * BLK + offsets

time: 689 us -> 746 us (1.083)
  the two profiles are of different devices: /device:TPU:20 before, /device:TPU:32 now
where the time goes in v1:
time: 746 us; the launch traced here: 739 us
  matrix products  295 us (40%)
  waiting for transfers between devices  263 us (35%)
  local copies, waits for them, and re-layouts  138 us (18%)
  other arithmetic  23.5 us (3%)
  starting transfers between devices  17.4 us (2%)
    all_to_all x2, waiting for transfers between devices, local(): lax.all_to_all(placed.astype(jnp.bfloat16).reshape(groups_count, MOST, pa...  164 us
    dot_general x16, matrix products, add_block(): jnp.dot(real_slice, cos_part, preferred_element_type=jnp.float32)  146 us
    dot_general x16, matrix products, add_block(): jnp.dot(imag_slice, sin_part, preferred_element_type=jnp.float32)  143 us
    ppermute x7, waiting for transfers between devices, local(): lax.ppermute(ring[-1], 'chan', [(dev, (dev + 1) % 8) for dev in range(8)])  99.1 us
    unnamed x44, local copies, waits for them, and re-layouts  32.9 us
    dynamic_slice x2, local copies, waits for them, and re-layouts, local(): jnp.roll(jnp.concatenate(ring[::-1], axis=0), (lax.axis_index('chan') + 1...  24 us
    convert_element_type x2, local copies, waits for them, and re-layouts, local(): placed.astype(jnp.bfloat16).reshape(groups_count, MOST, pairs, 2, F)  22 us
    all_to_all x2, starting transfers between devices, local(): lax.all_to_all(placed.astype(jnp.bfloat16).reshape(groups_count, MOST, pa...  17.4 us
  transfers between devices with their start and end apart: 9, of which 9 were waited for; matrix products, arithmetic and copies ran while one was open for 2% of the time, Pallas kernels for 0%

profile of v1, /device:TPU:32, one launch (start us, length us, event | category | flops | bytes accessed | tf_op | source)
XLA Modules:
  0.0 738.6 jit_solution(8948296364902445074)
XLA Ops:
  3.7 14.2 %collective-permute-done = bf16[16,2,2,8192]{3,0,2,1:T(8,128)(2,1)S(1)} collective-permute-done((bf16[16,2,2,8192]{3,0,2,1:T(8,128)(2,1)S(1)}, bf16[16,2,2,8192]{3,0,2,1:T(8,128)(2,1)S(1)}, u32[]{:S(2)}, u32[]{:S(2)}) %collective-permute-start) | collective-permute-done | bytes 1048608 | tf_op jit(solution)/shard_map/ppermute | solution.py:67
  17.9 14.2 %collective-permute-done.1 = bf16[16,2,2,8192]{3,0,2,1:T(8,128)(2,1)S(1)} collective-permute-done((bf16[16,2,2,8192]{3,0,2,1:T(8,128)(2,1)S(1)}, bf16[16,2,2,8192]{3,0,2,1:T(8,128)(2,1)S(1)}, u32[]{:S(2)}, u32[]{:S(2)}) %collective-permute-start.1) | collective-permute-done | bytes 1048608 | tf_op jit(solution)/shard_map/ppermute | solution.py:67
  33.2 14.2 %collective-permute-done.2 = bf16[16,2,2,8192]{3,0,2,1:T(8,128)(2,1)S(1)} collective-permute-done((bf16[16,2,2,8192]{3,0,2,1:T(8,128)(2,1)S(1)}, bf16[16,2,2,8192]{3,0,2,1:T(8,128)(2,1)S(1)}, u32[]{:S(2)}, u32[]{:S(2)}) %collective-permute-start.2) | collective-permute-done | bytes 1048608 | tf_op jit(solution)/shard_map/ppermute | solution.py:67
  48.4 14.2 %collective-permute-done.3 = bf16[16,2,2,8192]{3,0,2,1:T(8,128)(2,1)S(1)} collective-permute-done((bf16[16,2,2,8192]{3,0,2,1:T(8,128)(2,1)S(1)}, bf16[16,2,2,8192]{3,0,2,1:T(8,128)(2,1)S(1)}, u32[]{:S(2)}, u32[]{:S(2)}) %collective-permute-start.3) | collective-permute-done | bytes 1048608 | tf_op jit(solution)/shard_map/ppermute | solution.py:67
  63.6 14.2 %collective-permute-done.4 = bf16[16,2,2,8192]{3,0,2,1:T(8,128)(2,1)S(1)} collective-permute-done((bf16[16,2,2,8192]{3,0,2,1:T(8,128)(2,1)S(1)}, bf16[16,2,2,8192]{3,0,2,1:T(8,128)(2,1)S(1)}, u32[]{:S(2)}, u32[]{:S(2)}) %collective-permute-start.4) | collective-permute-done | bytes 1048608 | tf_op jit(solution)/shard_map/ppermute | solution.py:67
  78.8 14.3 %collective-permute-done.5 = bf16[16,2,2,8192]{3,0,2,1:T(8,128)(2,1)} collective-permute-done((bf16[16,2,2,8192]{3,0,2,1:T(8,128)(2,1)S(1)}, bf16[16,2,2,8192]{3,0,2,1:T(8,128)(2,1)}, u32[]{:S(2)}, u32[]{:S(2)}) %collective-permute-start.5) | collective-permute-done | bytes 1048608 | tf_op jit(solution)/shard_map/ppermute | solution.py:67
  94.0 13.6 %collective-permute-done.6 = bf16[16,2,2,8192]{3,0,2,1:T(8,128)(2,1)} collective-permute-done((bf16[16,2,2,8192]{3,0,2,1:T(8,128)(2,1)}, bf16[16,2,2,8192]{3,0,2,1:T(8,128)(2,1)}, u32[]{:S(2)}, u32[]{:S(2)}) %collective-permute-start.6) | collective-permute-done | bytes 1048608 | tf_op jit(solution)/shard_map/ppermute | solution.py:67
  107.7 2.2 constant_dynamic-update-slice_fusion.15
  109.9 2.3 constant_dynamic-update-slice_fusion.14
  118.9 2.2 constant_dynamic-update-slice_fusion.7
  121.1 2.2 constant_dynamic-update-slice_fusion.6
  130.1 7.6 %constant_dynamic-slice_fusion = bf16[128,2,2,8192]{3,0,2,1:T(8,128)(2,1)} fusion(bf16[256,2,2,8192]{3,0,2,1:T(8,128)(2,1)} %constant_dynamic-update-slice_fusion, s32[]{:T(128)S(6)} %select_n.66), kind=kLoop, calls=%fused_computation.91 | loop fusion | bytes 16777220 | tf_op jit(solution)/shard_map/jit(_roll_dynamic)/dynamic_slice | solution.py:68
  137.7 16.3 %copy.41 = bf16[128,2,2,8192]{3,2,1,0:T(2,128)(2,1)} copy(bf16[128,2,2,8192]{3,0,2,1:T(8,128)(2,1)} %constant_dynamic-slice_fusion) | data formatting | bytes 16777216 | tf_op jit(solution)/shard_map/jit(_roll_dynamic)/dynamic_slice | solution.py:68
  154.0 11.3 %gather_fusion = bf16[36,2,2,8192]{3,2,1,0:T(2,128)(2,1)S(1)} fusion(bf16[128,2,2,8192]{3,2,1,0:T(2,128)(2,1)} %copy.41, s32[1024]{0:T(1024)S(1)} %pad_clamp_fusion.1), kind=kCustom, calls=%fused_computation.clone | custom fusion | bytes 4718736 | tf_op jit(solution)/shard_map/jit(_take)/gather | solution.py:75
  167.5 5.4 fusion.36
  172.9 3.2 copy.76
  176.1 3.3 copy.78
  179.4 11.5 %gather_fusion.1 = bf16[36,2,2,8192]{3,2,1,0:T(2,128)(2,1)S(1)} fusion(bf16[128,2,2,8192]{3,2,1,0:T(2,128)(2,1)} %copy.41, s32[1024]{0:T(1024)S(1)} %pad_clamp_fusion), kind=kCustom, calls=%fused_computation.1.clone | custom fusion | bytes 4718736 | tf_op jit(solution)/shard_map/jit(_take)/gather | solution.py:76
  193.0 5.4 fusion.37
  205.7 11.0 %copy.49 = bf16[48,4,2,8192]{3,2,1,0:T(2,128)(2,1)} copy(bf16[48,4,2,8192]{3,0,2,1:T(8,128)(2,1)S(1)} %convolution_convert_fusion.1) | data formatting | bytes 12582912 | tf_op jit(solution)/shard_map/convert_element_type | solution.py:94
  216.7 7.1 all-to-all-start
  223.8 3.3 convolution_convert_fusion
  227.1 11.0 %copy.50 = bf16[48,4,2,8192]{3,2,1,0:T(2,128)(2,1)} copy(bf16[48,4,2,8192]{3,0,2,1:T(8,128)(2,1)S(1)} %convolution_convert_fusion) | data formatting | bytes 12582912 | tf_op jit(solution)/shard_map/convert_element_type | solution.py:94
  238.1 85.4 %all-to-all-done = bf16[16,3,4,2,8192]{4,3,2,1,0:T(2,128)(2,1)} async-done(((bf16[16,3,4,2,8192]{4,3,2,1,0:T(2,128)(2,1)}), bf16[16,3,4,2,8192]{4,3,2,1,0:T(2,128)(2,1)}, u32[]{:S(2)}, u32[]{:S(2)}) %all-to-all-start) | async-done | bytes 6291488 | tf_op jit(solution)/shard_map/all_to_all | solution.py:93
  323.5 10.3 %all-to-all-start.1 = ((bf16[16,3,4,2,8192]{4,3,2,1,0:T(2,128)(2,1)}), bf16[16,3,4,2,8192]{4,3,2,1,0:T(2,128)(2,1)}, u32[]{:S(2)}, u32[]{:S(2)}) async-start(bf16[16,3,4,2,8192]{4,3,2,1,0:T(2,128)(2,1)} %bitcast.51), calls=%async_computation.1 | async-start | bytes 12582912 | tf_op jit(solution)/shard_map/all_to_all | solution.py:93
  333.9 78.6 %all-to-all-done.1 = bf16[16,3,4,2,8192]{4,3,2,1,0:T(2,128)(2,1)} async-done(((bf16[16,3,4,2,8192]{4,3,2,1,0:T(2,128)(2,1)}), bf16[16,3,4,2,8192]{4,3,2,1,0:T(2,128)(2,1)}, u32[]{:S(2)}, u32[]{:S(2)}) %all-to-all-start.1) | async-done | bytes 6291488 | tf_op jit(solution)/shard_map/all_to_all | solution.py:93
  412.4 11.2 %multiply_convert_fusion.4 = bf16[16,3,4,2,8192]{4,3,2,1,0:T(2,128)(2,1)S(1)} fusion(bf16[16,3,4,2,8192]{4,3,2,1,0:T(2,128)(2,1)} %all-to-all-done.1, bf16[16,3,4,2,8192]{4,3,2,1,0:T(2,128)(2,1)} %all-to-all-done), kind=kLoop, calls=%fused_computation.29 | loop fusion | flops 15728640 | bytes 18874368 | tf_op jit(solution)/shard_map/convert_element_type | solution.py:100
  423.6 13.4 %fusion.35 = (bf16[192,1,8192]{2,1,0:T(2,128)(2,1)S(1)}, bf16[192,1,8192]{2,1,0:T(2,128)(2,1)S(1)}) fusion(bf16[192,2,8192]{2,1,0:T(2,128)(2,1)S(1)} %bitcast.46), kind=kLoop, calls=%fused_computation.94 | loop fusion | bytes 12582912 | tf_op jit(solution)/shard_map/slice | solution.py:28
  437.1 3.4 copy.73
  440.5 5.1 copy.74
  445.6 290.4 %while.16 = (s32[]{:T(128)}, f32[192,1024]{1,0:T(8,128)}, bf16[192,8192]{1,0:T(8,128)(2,1)}, bf16[192,8192]{1,0:T(8,128)(2,1)S(1)}, s32[]{:T(128)}, /*index=5*/s32[]{:T(128)}, s32[]{:T(128)}, s32[]{:T(128)}) while((s32[]{:T(128)}, f32[192,1024]{1,0:T(8,128)}, bf16[192,8192]{1,0:T(8,128)(2,1)}, bf16[192,8192]{1,0:T(8,128)(2,1)S(1)}, ...), condition=%wide.region_3.5_spmd.clone, body=%wide.region_2.4_spmd.clone.sunk | while | flops 420548096 | bytes 3563677 | solution.py:39
  445.8 8.9 %convolution_add_fusion.4 = f32[192,1024]{1,0:T(8,128)S(1)} fusion(f32[512]{0:T(512)S(1)} %select_multiply_fusion.2, s32[1024]{0:T(1024)S(1)} %iota_add_fusion.4, s32[512]{0:T(512)S(1)} %iota_add_fusion.5, f32[192,1024]{1,0:T(8,128)} %get-tuple-element.190, pred[]{:T(512)S(6)} %compare.5, bf16[192,8192]{1,0:T(8,128)(2,1)} %get-tuple-element.199, ...), kind=kOutput, calls=%fused_computation.13.clone.1 | convolution fusion | flops 210108416 | bytes 1777669 | tf_op jit(solution)/shard_map/while/body/eval_jaxpr/dot_general | solution.py:35
  454.7 9.0 %convolution_add_fusion.5 = f32[192,1024]{1,0:T(8,128)} fusion(f32[192,1024]{1,0:T(8,128)S(1)} %convolution_add_fusion.4, f32[512]{0:T(512)S(1)} %select_multiply_fusion.2, s32[1024]{0:T(1024)S(1)} %iota_add_fusion.4, s32[512]{0:T(512)S(1)} %iota_add_fusion.5, bf16[192,8192]{1,0:T(8,128)(2,1)S(1)} %get-tuple-element.200, s32[]{:T(128)S(6)} %select_n.107), kind=kOutput, calls=%fused_computation.12.clone.1 | convolution fusion | flops 210436096 | bytes 1777668 | tf_op jit(solution)/shard_map/while/body/eval_jaxpr/dot_general | solution.py:36
  463.7 9.2 %convolution_add_fusion.4 = f32[192,1024]{1,0:T(8,128)S(1)} fusion(f32[512]{0:T(512)S(1)} %select_multiply_fusion.2, s32[1024]{0:T(1024)S(1)} %iota_add_fusion.4, s32[512]{0:T(512)S(1)} %iota_add_fusion.5, f32[192,1024]{1,0:T(8,128)} %get-tuple-element.190, pred[]{:T(512)S(6)} %compare.5, bf16[192,8192]{1,0:T(8,128)(2,1)} %get-tuple-element.199, ...), kind=kOutput, calls=%fused_computation.13.clone.1 | convolution fusion | flops 210108416 | bytes 1777669 | tf_op jit(solution)/shard_map/while/body/eval_jaxpr/dot_general | solution.py:35
  472.9 9.0 %convolution_add_fusion.5 = f32[192,1024]{1,0:T(8,128)} fusion(f32[192,1024]{1,0:T(8,128)S(1)} %convolution_add_fusion.4, f32[512]{0:T(512)S(1)} %select_multiply_fusion.2, s32[1024]{0:T(1024)S(1)} %iota_add_fusion.4, s32[512]{0:T(512)S(1)} %iota_add_fusion.5, bf16[192,8192]{1,0:T(8,128)(2,1)S(1)} %get-tuple-element.200, s32[]{:T(128)S(6)} %select_n.107), kind=kOutput, calls=%fused_computation.12.clone.1 | convolution fusion | flops 210436096 | bytes 1777668 | tf_op jit(solution)/shard_map/while/body/eval_jaxpr/dot_general | solution.py:36
  481.8 9.2 %convolution_add_fusion.4 = f32[192,1024]{1,0:T(8,128)S(1)} fusion(f32[512]{0:T(512)S(1)} %select_multiply_fusion.2, s32[1024]{0:T(1024)S(1)} %iota_add_fusion.4, s32[512]{0:T(512)S(1)} %iota_add_fusion.5, f32[192,1024]{1,0:T(8,128)} %get-tuple-element.190, pred[]{:T(512)S(6)} %compare.5, bf16[192,8192]{1,0:T(8,128)(2,1)} %get-tuple-element.199, ...), kind=kOutput, calls=%fused_computation.13.clone.1 | convolution fusion | flops 210108416 | bytes 1777669 | tf_op jit(solution)/shard_map/while/body/eval_jaxpr/dot_general | solution.py:35
  491.0 9.0 %convolution_add_fusion.5 = f32[192,1024]{1,0:T(8,128)} fusion(f32[192,1024]{1,0:T(8,128)S(1)} %convolution_add_fusion.4, f32[512]{0:T(512)S(1)} %select_multiply_fusion.2, s32[1024]{0:T(1024)S(1)} %iota_add_fusion.4, s32[512]{0:T(512)S(1)} %iota_add_fusion.5, bf16[192,8192]{1,0:T(8,128)(2,1)S(1)} %get-tuple-element.200, s32[]{:T(128)S(6)} %select_n.107), kind=kOutput, calls=%fused_computation.12.clone.1 | convolution fusion | flops 210436096 | bytes 1777668 | tf_op jit(solution)/shard_map/while/body/eval_jaxpr/dot_general | solution.py:36
  500.0 9.2 %convolution_add_fusion.4 = f32[192,1024]{1,0:T(8,128)S(1)} fusion(f32[512]{0:T(512)S(1)} %select_multiply_fusion.2, s32[1024]{0:T(1024)S(1)} %iota_add_fusion.4, s32[512]{0:T(512)S(1)} %iota_add_fusion.5, f32[192,1024]{1,0:T(8,128)} %get-tuple-element.190, pred[]{:T(512)S(6)} %compare.5, bf16[192,8192]{1,0:T(8,128)(2,1)} %get-tuple-element.199, ...), kind=kOutput, calls=%fused_computation.13.clone.1 | convolution fusion | flops 210108416 | bytes 1777669 | tf_op jit(solution)/shard_map/while/body/eval_jaxpr/dot_general | solution.py:35
  509.2 9.0 %convolution_add_fusion.5 = f32[192,1024]{1,0:T(8,128)} fusion(f32[192,1024]{1,0:T(8,128)S(1)} %convolution_add_fusion.4, f32[512]{0:T(512)S(1)} %select_multiply_fusion.2, s32[1024]{0:T(1024)S(1)} %iota_add_fusion.4, s32[512]{0:T(512)S(1)} %iota_add_fusion.5, bf16[192,8192]{1,0:T(8,128)(2,1)S(1)} %get-tuple-element.200, s32[]{:T(128)S(6)} %select_n.107), kind=kOutput, calls=%fused_computation.12.clone.1 | convolution fusion | flops 210436096 | bytes 1777668 | tf_op jit(solution)/shard_map/while/body/eval_jaxpr/dot_general | solution.py:36
  518.2 9.2 %convolution_add_fusion.4 = f32[192,1024]{1,0:T(8,128)S(1)} fusion(f32[512]{0:T(512)S(1)} %select_multiply_fusion.2, s32[1024]{0:T(1024)S(1)} %iota_add_fusion.4, s32[512]{0:T(512)S(1)} %iota_add_fusion.5, f32[192,1024]{1,0:T(8,128)} %get-tuple-element.190, pred[]{:T(512)S(6)} %compare.5, bf16[192,8192]{1,0:T(8,128)(2,1)} %get-tuple-element.199, ...), kind=kOutput, calls=%fused_computation.13.clone.1 | convolution fusion | flops 210108416 | bytes 1777669 | tf_op jit(solution)/shard_map/while/body/eval_jaxpr/dot_general | solution.py:35
  527.3 9.0 %convolution_add_fusion.5 = f32[192,1024]{1,0:T(8,128)} fusion(f32[192,1024]{1,0:T(8,128)S(1)} %convolution_add_fusion.4, f32[512]{0:T(512)S(1)} %select_multiply_fusion.2, s32[1024]{0:T(1024)S(1)} %iota_add_fusion.4, s32[512]{0:T(512)S(1)} %iota_add_fusion.5, bf16[192,8192]{1,0:T(8,128)(2,1)S(1)} %get-tuple-element.200, s32[]{:T(128)S(6)} %select_n.107), kind=kOutput, calls=%fused_computation.12.clone.1 | convolution fusion | flops 210436096 | bytes 1777668 | tf_op jit(solution)/shard_map/while/body/eval_jaxpr/dot_general | solution.py:36
  536.3 9.2 %convolution_add_fusion.4 = f32[192,1024]{1,0:T(8,128)S(1)} fusion(f32[512]{0:T(512)S(1)} %select_multiply_fusion.2, s32[1024]{0:T(1024)S(1)} %iota_add_fusion.4, s32[512]{0:T(512)S(1)} %iota_add_fusion.5, f32[192,1024]{1,0:T(8,128)} %get-tuple-element.190, pred[]{:T(512)S(6)} %compare.5, bf16[192,8192]{1,0:T(8,128)(2,1)} %get-tuple-element.199, ...), kind=kOutput, calls=%fused_computation.13.clone.1 | convolution fusion | flops 210108416 | bytes 1777669 | tf_op jit(solution)/shard_map/while/body/eval_jaxpr/dot_general | solution.py:35
  545.5 9.0 %convolution_add_fusion.5 = f32[192,1024]{1,0:T(8,128)} fusion(f32[192,1024]{1,0:T(8,128)S(1)} %convolution_add_fusion.4, f32[512]{0:T(512)S(1)} %select_multiply_fusion.2, s32[1024]{0:T(1024)S(1)} %iota_add_fusion.4, s32[512]{0:T(512)S(1)} %iota_add_fusion.5, bf16[192,8192]{1,0:T(8,128)(2,1)S(1)} %get-tuple-element.200, s32[]{:T(128)S(6)} %select_n.107), kind=kOutput, calls=%fused_computation.12.clone.1 | convolution fusion | flops 210436096 | bytes 1777668 | tf_op jit(solution)/shard_map/while/body/eval_jaxpr/dot_general | solution.py:36
  554.5 9.2 %convolution_add_fusion.4 = f32[192,1024]{1,0:T(8,128)S(1)} fusion(f32[512]{0:T(512)S(1)} %select_multiply_fusion.2, s32[1024]{0:T(1024)S(1)} %iota_add_fusion.4, s32[512]{0:T(512)S(1)} %iota_add_fusion.5, f32[192,1024]{1,0:T(8,128)} %get-tuple-element.190, pred[]{:T(512)S(6)} %compare.5, bf16[192,8192]{1,0:T(8,128)(2,1)} %get-tuple-element.199, ...), kind=kOutput, calls=%fused_computation.13.clone.1 | convolution fusion | flops 210108416 | bytes 1777669 | tf_op jit(solution)/shard_map/while/body/eval_jaxpr/dot_general | solution.py:35
  563.6 9.0 %convolution_add_fusion.5 = f32[192,1024]{1,0:T(8,128)} fusion(f32[192,1024]{1,0:T(8,128)S(1)} %convolution_add_fusion.4, f32[512]{0:T(512)S(1)} %select_multiply_fusion.2, s32[1024]{0:T(1024)S(1)} %iota_add_fusion.4, s32[512]{0:T(512)S(1)} %iota_add_fusion.5, bf16[192,8192]{1,0:T(8,128)(2,1)S(1)} %get-tuple-element.200, s32[]{:T(128)S(6)} %select_n.107), kind=kOutput, calls=%fused_computation.12.clone.1 | convolution fusion | flops 210436096 | bytes 1777668 | tf_op jit(solution)/shard_map/while/body/eval_jaxpr/dot_general | solution.py:36
  572.6 9.2 %convolution_add_fusion.4 = f32[192,1024]{1,0:T(8,128)S(1)} fusion(f32[512]{0:T(512)S(1)} %select_multiply_fusion.2, s32[1024]{0:T(1024)S(1)} %iota_add_fusion.4, s32[512]{0:T(512)S(1)} %iota_add_fusion.5, f32[192,1024]{1,0:T(8,128)} %get-tuple-element.190, pred[]{:T(512)S(6)} %compare.5, bf16[192,8192]{1,0:T(8,128)(2,1)} %get-tuple-element.199, ...), kind=kOutput, calls=%fused_computation.13.clone.1 | convolution fusion | flops 210108416 | bytes 1777669 | tf_op jit(solution)/shard_map/while/body/eval_jaxpr/dot_general | solution.py:35
  581.8 9.0 %convolution_add_fusion.5 = f32[192,1024]{1,0:T(8,128)} fusion(f32[192,1024]{1,0:T(8,128)S(1)} %convolution_add_fusion.4, f32[512]{0:T(512)S(1)} %select_multiply_fusion.2, s32[1024]{0:T(1024)S(1)} %iota_add_fusion.4, s32[512]{0:T(512)S(1)} %iota_add_fusion.5, bf16[192,8192]{1,0:T(8,128)(2,1)S(1)} %get-tuple-element.200, s32[]{:T(128)S(6)} %select_n.107), kind=kOutput, calls=%fused_computation.12.clone.1 | convolution fusion | flops 210436096 | bytes 1777668 | tf_op jit(solution)/shard_map/while/body/eval_jaxpr/dot_general | solution.py:36
  590.8 9.2 %convolution_add_fusion.4 = f32[192,1024]{1,0:T(8,128)S(1)} fusion(f32[512]{0:T(512)S(1)} %select_multiply_fusion.2, s32[1024]{0:T(1024)S(1)} %iota_add_fusion.4, s32[512]{0:T(512)S(1)} %iota_add_fusion.5, f32[192,1024]{1,0:T(8,128)} %get-tuple-element.190, pred[]{:T(512)S(6)} %compare.5, bf16[192,8192]{1,0:T(8,128)(2,1)} %get-tuple-element.199, ...), kind=kOutput, calls=%fused_computation.13.clone.1 | convolution fusion | flops 210108416 | bytes 1777669 | tf_op jit(solution)/shard_map/while/body/eval_jaxpr/dot_general | solution.py:35
  600.0 9.0 %convolution_add_fusion.5 = f32[192,1024]{1,0:T(8,128)} fusion(f32[192,1024]{1,0:T(8,128)S(1)} %convolution_add_fusion.4, f32[512]{0:T(512)S(1)} %select_multiply_fusion.2, s32[1024]{0:T(1024)S(1)} %iota_add_fusion.4, s32[512]{0:T(512)S(1)} %iota_add_fusion.5, bf16[192,8192]{1,0:T(8,128)(2,1)S(1)} %get-tuple-element.200, s32[]{:T(128)S(6)} %select_n.107), kind=kOutput, calls=%fused_computation.12.clone.1 | convolution fusion | flops 210436096 | bytes 1777668 | tf_op jit(solution)/shard_map/while/body/eval_jaxpr/dot_general | solution.py:36
  608.9 9.2 %convolution_add_fusion.4 = f32[192,1024]{1,0:T(8,128)S(1)} fusion(f32[512]{0:T(512)S(1)} %select_multiply_fusion.2, s32[1024]{0:T(1024)S(1)} %iota_add_fusion.4, s32[512]{0:T(512)S(1)} %iota_add_fusion.5, f32[192,1024]{1,0:T(8,128)} %get-tuple-element.190, pred[]{:T(512)S(6)} %compare.5, bf16[192,8192]{1,0:T(8,128)(2,1)} %get-tuple-element.199, ...), kind=kOutput, calls=%fused_computation.13.clone.1 | convolution fusion | flops 210108416 | bytes 1777669 | tf_op jit(solution)/shard_map/while/body/eval_jaxpr/dot_general | solution.py:35
  618.1 9.0 %convolution_add_fusion.5 = f32[192,1024]{1,0:T(8,128)} fusion(f32[192,1024]{1,0:T(8,128)S(1)} %convolution_add_fusion.4, f32[512]{0:T(512)S(1)} %select_multiply_fusion.2, s32[1024]{0:T(1024)S(1)} %iota_add_fusion.4, s32[512]{0:T(512)S(1)} %iota_add_fusion.5, bf16[192,8192]{1,0:T(8,128)(2,1)S(1)} %get-tuple-element.200, s32[]{:T(128)S(6)} %select_n.107), kind=kOutput, calls=%fused_computation.12.clone.1 | convolution fusion | flops 210436096 | bytes 1777668 | tf_op jit(solution)/shard_map/while/body/eval_jaxpr/dot_general | solution.py:36
  627.1 9.2 %convolution_add_fusion.4 = f32[192,1024]{1,0:T(8,128)S(1)} fusion(f32[512]{0:T(512)S(1)} %select_multiply_fusion.2, s32[1024]{0:T(1024)S(1)} %iota_add_fusion.4, s32[512]{0:T(512)S(1)} %iota_add_fusion.5, f32[192,1024]{1,0:T(8,128)} %get-tuple-element.190, pred[]{:T(512)S(6)} %compare.5, bf16[192,8192]{1,0:T(8,128)(2,1)} %get-tuple-element.199, ...), kind=kOutput, calls=%fused_computation.13.clone.1 | convolution fusion | flops 210108416 | bytes 1777669 | tf_op jit(solution)/shard_map/while/body/eval_jaxpr/dot_general | solution.py:35
  636.3 9.0 %convolution_add_fusion.5 = f32[192,1024]{1,0:T(8,128)} fusion(f32[192,1024]{1,0:T(8,128)S(1)} %convolution_add_fusion.4, f32[512]{0:T(512)S(1)} %select_multiply_fusion.2, s32[1024]{0:T(1024)S(1)} %iota_add_fusion.4, s32[512]{0:T(512)S(1)} %iota_add_fusion.5, bf16[192,8192]{1,0:T(8,128)(2,1)S(1)} %get-tuple-element.200, s32[]{:T(128)S(6)} %select_n.107), kind=kOutput, calls=%fused_computation.12.clone.1 | convolution fusion | flops 210436096 | bytes 1777668 | tf_op jit(solution)/shard_map/while/body/eval_jaxpr/dot_general | solution.py:36
  645.2 9.2 %convolution_add_fusion.4 = f32[192,1024]{1,0:T(8,128)S(1)} fusion(f32[512]{0:T(512)S(1)} %select_multiply_fusion.2, s32[1024]{0:T(1024)S(1)} %iota_add_fusion.4, s32[512]{0:T(512)S(1)} %iota_add_fusion.5, f32[192,1024]{1,0:T(8,128)} %get-tuple-element.190, pred[]{:T(512)S(6)} %compare.5, bf16[192,8192]{1,0:T(8,128)(2,1)} %get-tuple-element.199, ...), kind=kOutput, calls=%fused_computation.13.clone.1 | convolution fusion | flops 210108416 | bytes 1777669 | tf_op jit(solution)/shard_map/while/body/eval_jaxpr/dot_general | solution.py:35
  654.4 9.0 %convolution_add_fusion.5 = f32[192,1024]{1,0:T(8,128)} fusion(f32[192,1024]{1,0:T(8,128)S(1)} %convolution_add_fusion.4, f32[512]{0:T(512)S(1)} %select_multiply_fusion.2, s32[1024]{0:T(1024)S(1)} %iota_add_fusion.4, s32[512]{0:T(512)S(1)} %iota_add_fusion.5, bf16[192,8192]{1,0:T(8,128)(2,1)S(1)} %get-tuple-element.200, s32[]{:T(128)S(6)} %select_n.107), kind=kOutput, calls=%fused_computation.12.clone.1 | convolution fusion | flops 210436096 | bytes 1777668 | tf_op jit(solution)/shard_map/while/body/eval_jaxpr/dot_general | solution.py:36
  663.4 9.2 %convolution_add_fusion.4 = f32[192,1024]{1,0:T(8,128)S(1)} fusion(f32[512]{0:T(512)S(1)} %select_multiply_fusion.2, s32[1024]{0:T(1024)S(1)} %iota_add_fusion.4, s32[512]{0:T(512)S(1)} %iota_add_fusion.5, f32[192,1024]{1,0:T(8,128)} %get-tuple-element.190, pred[]{:T(512)S(6)} %compare.5, bf16[192,8192]{1,0:T(8,128)(2,1)} %get-tuple-element.199, ...), kind=kOutput, calls=%fused_computation.13.clone.1 | convolution fusion | flops 210108416 | bytes 1777669 | tf_op jit(solution)/shard_map/while/body/eval_jaxpr/dot_general | solution.py:35
  672.6 9.0 %convolution_add_fusion.5 = f32[192,1024]{1,0:T(8,128)} fusion(f32[192,1024]{1,0:T(8,128)S(1)} %convolution_add_fusion.4, f32[512]{0:T(512)S(1)} %select_multiply_fusion.2, s32[1024]{0:T(1024)S(1)} %iota_add_fusion.4, s32[512]{0:T(512)S(1)} %iota_add_fusion.5, bf16[192,8192]{1,0:T(8,128)(2,1)S(1)} %get-tuple-element.200, s32[]{:T(128)S(6)} %select_n.107), kind=kOutput, calls=%fused_computation.12.clone.1 | convolution fusion | flops 210436096 | bytes 1777668 | tf_op jit(solution)/shard_map/while/body/eval_jaxpr/dot_general | solution.py:36
  681.6 9.2 %convolution_add_fusion.4 = f32[192,1024]{1,0:T(8,128)S(1)} fusion(f32[512]{0:T(512)S(1)} %select_multiply_fusion.2, s32[1024]{0:T(1024)S(1)} %iota_add_fusion.4, s32[512]{0:T(512)S(1)} %iota_add_fusion.5, f32[192,1024]{1,0:T(8,128)} %get-tuple-element.190, pred[]{:T(512)S(6)} %compare.5, bf16[192,8192]{1,0:T(8,128)(2,1)} %get-tuple-element.199, ...), kind=kOutput, calls=%fused_computation.13.clone.1 | convolution fusion | flops 210108416 | bytes 1777669 | tf_op jit(solution)/shard_map/while/body/eval_jaxpr/dot_general | solution.py:35
  690.7 9.0 %convolution_add_fusion.5 = f32[192,1024]{1,0:T(8,128)} fusion(f32[192,1024]{1,0:T(8,128)S(1)} %convolution_add_fusion.4, f32[512]{0:T(512)S(1)} %select_multiply_fusion.2, s32[1024]{0:T(1024)S(1)} %iota_add_fusion.4, s32[512]{0:T(512)S(1)} %iota_add_fusion.5, bf16[192,8192]{1,0:T(8,128)(2,1)S(1)} %get-tuple-element.200, s32[]{:T(128)S(6)} %select_n.107), kind=kOutput, calls=%fused_computation.12.clone.1 | convolution fusion | flops 210436096 | bytes 1777668 | tf_op jit(solution)/shard_map/while/body/eval_jaxpr/dot_general | solution.py:36
  699.7 9.2 %convolution_add_fusion.4 = f32[192,1024]{1,0:T(8,128)S(1)} fusion(f32[512]{0:T(512)S(1)} %select_multiply_fusion.2, s32[1024]{0:T(1024)S(1)} %iota_add_fusion.4, s32[512]{0:T(512)S(1)} %iota_add_fusion.5, f32[192,1024]{1,0:T(8,128)} %get-tuple-element.190, pred[]{:T(512)S(6)} %compare.5, bf16[192,8192]{1,0:T(8,128)(2,1)} %get-tuple-element.199, ...), kind=kOutput, calls=%fused_computation.13.clone.1 | convolution fusion | flops 210108416 | bytes 1777669 | tf_op jit(solution)/shard_map/while/body/eval_jaxpr/dot_general | solution.py:35
  708.9 9.0 %convolution_add_fusion.5 = f32[192,1024]{1,0:T(8,128)} fusion(f32[192,1024]{1,0:T(8,128)S(1)} %convolution_add_fusion.4, f32[512]{0:T(512)S(1)} %select_multiply_fusion.2, s32[1024]{0:T(1024)S(1)} %iota_add_fusion.4, s32[512]{0:T(512)S(1)} %iota_add_fusion.5, bf16[192,8192]{1,0:T(8,128)(2,1)S(1)} %get-tuple-element.200, s32[]{:T(128)S(6)} %select_n.107), kind=kOutput, calls=%fused_computation.12.clone.1 | convolution fusion | flops 210436096 | bytes 1777668 | tf_op jit(solution)/shard_map/while/body/eval_jaxpr/dot_general | solution.py:36
  717.9 9.2 %convolution_add_fusion.4 = f32[192,1024]{1,0:T(8,128)S(1)} fusion(f32[512]{0:T(512)S(1)} %select_multiply_fusion.2, s32[1024]{0:T(1024)S(1)} %iota_add_fusion.4, s32[512]{0:T(512)S(1)} %iota_add_fusion.5, f32[192,1024]{1,0:T(8,128)} %get-tuple-element.190, pred[]{:T(512)S(6)} %compare.5, bf16[192,8192]{1,0:T(8,128)(2,1)} %get-tuple-element.199, ...), kind=kOutput, calls=%fused_computation.13.clone.1 | convolution fusion | flops 210108416 | bytes 1777669 | tf_op jit(solution)/shard_map/while/body/eval_jaxpr/dot_general | solution.py:35
  727.0 9.0 %convolution_add_fusion.5 = f32[192,1024]{1,0:T(8,128)} fusion(f32[192,1024]{1,0:T(8,128)S(1)} %convolution_add_fusion.4, f32[512]{0:T(512)S(1)} %select_multiply_fusion.2, s32[1024]{0:T(1024)S(1)} %iota_add_fusion.4, s32[512]{0:T(512)S(1)} %iota_add_fusion.5, bf16[192,8192]{1,0:T(8,128)(2,1)S(1)} %get-tuple-element.200, s32[]{:T(128)S(6)} %select_n.107), kind=kOutput, calls=%fused_computation.12.clone.1 | convolution fusion | flops 210436096 | bytes 1777668 | tf_op jit(solution)/shard_map/while/body/eval_jaxpr/dot_general | solution.py:36
  736.0 2.2 reshape_reshape.3
  (120 shorter events, 33.5 us)
Async XLA Ops:
  1.8 1.2 copy-start.1
  2.1 91.0 %copy-start.12 = (s32[1,1,18,2]{2,3,1,0:T(2,128)S(1)}, s32[1,1,18,2]{2,3,1,0:T(2,128)}, u32[]{:S(2)}) copy-start(s32[1,1,18,2]{2,3,1,0:T(2,128)} %param.8) | copy-start | bytes 436
  2.1 91.7 %copy-start.13 = (s32[1,1,18,1]{2,3,1,0:T(1,128)S(1)}, s32[1,1,18,1]{2,3,1,0:T(1,128)}, u32[]{:S(2)}) copy-start(s32[1,1,18,1]{2,3,1,0:T(1,128)} %param.9) | copy-start | bytes 220
  3.7 14.2 %collective-permute-start = (bf16[16,2,2,8192]{3,0,2,1:T(8,128)(2,1)S(1)}, bf16[16,2,2,8192]{3,0,2,1:T(8,128)(2,1)S(1)}, u32[]{:S(2)}, u32[]{:S(2)}) collective-permute-start(bf16[16,2,2,8192]{3,0,2,1:T(8,128)(2,1)S(1)} %multiply_convert_fusion.5), channel_id=1, source_target_pairs={{0,1},{1,2},{2,3},{3,4},{4,5},{5,6},{6,7},{7,0},{8,9},{9,10},{10,1... | collective-permute-start | bytes 3145736 | tf_op jit(solution)/shard_map/ppermute | solution.py:67
  17.9 14.2 %collective-permute-start.1 = (bf16[16,2,2,8192]{3,0,2,1:T(8,128)(2,1)S(1)}, bf16[16,2,2,8192]{3,0,2,1:T(8,128)(2,1)S(1)}, u32[]{:S(2)}, u32[]{:S(2)}) collective-permute-start(bf16[16,2,2,8192]{3,0,2,1:T(8,128)(2,1)S(1)} %collective-permute-done), channel_id=1, source_target_pairs={{0,1},{1,2},{2,3},{3,4},{4,5},{5,6},{6,7},{7,0},{8,9},{9,10},{10,1... | collective-permute-start | bytes 3145736 | tf_op jit(solution)/shard_map/ppermute | solution.py:67
  32.2 1.0 copy-start.4
  33.2 14.2 %collective-permute-start.2 = (bf16[16,2,2,8192]{3,0,2,1:T(8,128)(2,1)S(1)}, bf16[16,2,2,8192]{3,0,2,1:T(8,128)(2,1)S(1)}, u32[]{:S(2)}, u32[]{:S(2)}) collective-permute-start(bf16[16,2,2,8192]{3,0,2,1:T(8,128)(2,1)S(1)} %collective-permute-done.1), channel_id=1, source_target_pairs={{0,1},{1,2},{2,3},{3,4},{4,5},{5,6},{6,7},{7,0},{8,9},{9,10},{10,1... | collective-permute-start | bytes 3145736 | tf_op jit(solution)/shard_map/ppermute | solution.py:67
  47.4 1.0 copy-start.6
  48.4 14.2 %collective-permute-start.3 = (bf16[16,2,2,8192]{3,0,2,1:T(8,128)(2,1)S(1)}, bf16[16,2,2,8192]{3,0,2,1:T(8,128)(2,1)S(1)}, u32[]{:S(2)}, u32[]{:S(2)}) collective-permute-start(bf16[16,2,2,8192]{3,0,2,1:T(8,128)(2,1)S(1)} %collective-permute-done.2), channel_id=1, source_target_pairs={{0,1},{1,2},{2,3},{3,4},{4,5},{5,6},{6,7},{7,0},{8,9},{9,10},{10,1... | collective-permute-start | bytes 3145736 | tf_op jit(solution)/shard_map/ppermute | solution.py:67
  62.6 1.0 copy-start.8
  63.6 14.2 %collective-permute-start.4 = (bf16[16,2,2,8192]{3,0,2,1:T(8,128)(2,1)S(1)}, bf16[16,2,2,8192]{3,0,2,1:T(8,128)(2,1)S(1)}, u32[]{:S(2)}, u32[]{:S(2)}) collective-permute-start(bf16[16,2,2,8192]{3,0,2,1:T(8,128)(2,1)S(1)} %collective-permute-done.3), channel_id=1, source_target_pairs={{0,1},{1,2},{2,3},{3,4},{4,5},{5,6},{6,7},{7,0},{8,9},{9,10},{10,1... | collective-permute-start | bytes 3145736 | tf_op jit(solution)/shard_map/ppermute | solution.py:67
  77.8 1.0 copy-start.10
  78.8 14.3 %collective-permute-start.5 = (bf16[16,2,2,8192]{3,0,2,1:T(8,128)(2,1)S(1)}, bf16[16,2,2,8192]{3,0,2,1:T(8,128)(2,1)}, u32[]{:S(2)}, u32[]{:S(2)}) collective-permute-start(bf16[16,2,2,8192]{3,0,2,1:T(8,128)(2,1)S(1)} %collective-permute-done.4), channel_id=1, source_target_pairs={{0,1},{1,2},{2,3},{3,4},{4,5},{5,6},{6,7},{7,0},{8,9},{9,10},{10,1... | collective-permute-start | bytes 3145736 | tf_op jit(solution)/shard_map/ppermute | solution.py:67
  93.1 14.5 %collective-permute-start.6 = (bf16[16,2,2,8192]{3,0,2,1:T(8,128)(2,1)}, bf16[16,2,2,8192]{3,0,2,1:T(8,128)(2,1)}, u32[]{:S(2)}, u32[]{:S(2)}) collective-permute-start(bf16[16,2,2,8192]{3,0,2,1:T(8,128)(2,1)} %collective-permute-done.5), channel_id=1, source_target_pairs={{0,1},{1,2},{2,3},{3,4},{4,5},{5,6},{6,7},{7,0},{8,9},{9,10},{10,1... | collective-permute-start | bytes 3145736 | tf_op jit(solution)/shard_map/ppermute | solution.py:67
  93.8 18.5 %copy-start.11 = (bf16[16,2,2,8192]{3,0,2,1:T(8,128)(2,1)S(1)}, bf16[16,2,2,8192]{3,0,2,1:T(8,128)(2,1)}, u32[]{:S(2)}) copy-start(bf16[16,2,2,8192]{3,0,2,1:T(8,128)(2,1)} %copy-done.10) | copy-start | bytes 3145732
  94.0 19.3 %copy-start.9 = (bf16[16,2,2,8192]{3,0,2,1:T(8,128)(2,1)S(1)}, bf16[16,2,2,8192]{3,0,2,1:T(8,128)(2,1)}, u32[]{:S(2)}) copy-start(bf16[16,2,2,8192]{3,0,2,1:T(8,128)(2,1)} %copy-done.8) | copy-start | bytes 3145732
  109.9 4.4 copy-start.7
  112.2 3.1 copy-start.5
  198.4 3.1 copy-start.3
  199.9 2.0 copy-start.2
  203.4 2.2 copy-start
  216.7 106.8 %all-to-all-start = ((bf16[16,3,4,2,8192]{4,3,2,1,0:T(2,128)(2,1)}), bf16[16,3,4,2,8192]{4,3,2,1,0:T(2,128)(2,1)}, u32[]{:S(2)}, u32[]{:S(2)}) async-start(bf16[16,3,4,2,8192]{4,3,2,1,0:T(2,128)(2,1)} %bitcast.52), calls=%async_computation | async-start | bytes 12582912 | tf_op jit(solution)/shard_map/all_to_all | solution.py:93
  323.5 88.9 %all-to-all-start.1 = ((bf16[16,3,4,2,8192]{4,3,2,1,0:T(2,128)(2,1)}), bf16[16,3,4,2,8192]{4,3,2,1,0:T(2,128)(2,1)}, u32[]{:S(2)}, u32[]{:S(2)}) async-start(bf16[16,3,4,2,8192]{4,3,2,1,0:T(2,128)(2,1)} %bitcast.51), calls=%async_computation.1 | async-start | bytes 12582912 | tf_op jit(solution)/shard_map/all_to_all | solution.py:93
